TPU v7x, 32 devices: a whole 2x2x4 slice. The times are simulated.
32 devices in a mesh: grp: 2 (over y), seq: 4 (over z), head: 4 (over x, core).
Axes of the slice: x: 2, y: 2, z: 4, core: 2. Of those that a mesh axis runs over, the one named last changes fastest.
Arguments:
- tokens: bfloat16 [1024, 2048], P(('grp', 'seq')), parts along dimension 0, may hold values from -6 to 6
- attn_weight: bfloat16 [4, 2048, 2048], P(None, 'seq', 'head'), may hold values from -0.125 to 0.125
- attn_gain: float32 [2048], replicated, may hold values from 0.25 to 1.75
- moe_gain: float32 [2048], replicated, may hold values from 0.25 to 1.75
- routes: int32 [1024, 8], P(('grp', 'seq')), parts along dimension 0, may hold values from 0 to 63, all different within a row; in each aligned block of 128 rows (0 to 127, 128 to 255, ...) at most 18 rows name the same one
- gates: float32 [1024, 8], P(('grp', 'seq')), parts along dimension 0, may hold values from 0.05 to 0.4
- expert_gate: bfloat16 [64, 2048, 1024], P('seq', None, 'head'), may hold values from -0.125 to 0.125
- expert_up: bfloat16 [64, 2048, 1024], P('seq', None, 'head'), may hold values from -0.125 to 0.125
- expert_down: bfloat16 [64, 1024, 2048], P('seq', 'head'), may hold values from -0.1875 to 0.1875
Outputs:
- mixed: bfloat16 [1024, 2048], P(('grp', 'seq')), parts along dimension 0
There are 2 independent parts, one for each index of `grp`. A program takes and returns all parts, laid end to end along the dimension named above; an argument that names none is the same for every part. Nothing has to cross between parts.
Inputs may be any that keep to these rules, and one draw needn't show every extreme that they name: `routes`: in each aligned block of 128 tokens, no expert is named by more than 18 pairs of a token and a choice, a bound that some block reaches; a token's 8 experts differ.
All inputs are finite; a program needn't handle non-finite values.
Results may differ from a plain program's by a relative error of at most 0.015.
Values may be sent and summed in bfloat16 or wider, within the bound.
A program may use at most 128 MiB of HBM per device.

v0:
```python
import jax
import jax.numpy as jnp
from jax import lax
from jax.sharding import PartitionSpec as P

HEAD_DIM = 128
EXPERTS = 64
TOPK = 8
CAP = 18


PRECISE = lax.Precision.HIGHEST


def prefix_2(array, axis, combine, identity):
    peers, position = (lax.axis_size(axis), lax.axis_index(axis))
    everything = lax.all_gather(array.astype(jnp.bfloat16), axis)
    start = jnp.broadcast_to(jnp.asarray(identity, array.dtype), array.shape)

    def hop(k, before):
        reached = k < position
        new = combine(before, everything[k].astype(array.dtype))
        return jnp.where(reached, new, before)

    return lax.fori_loop(0, peers, hop, start)


def rms_scale(row_block, gain_vec):
    widened = row_block.astype(jnp.float32)
    factor = lax.rsqrt(jnp.mean(widened * widened, axis=-1, keepdims=True) + 1e-06)
    return widened * factor * gain_vec


def head_norm(outputs):
    return outputs * lax.rsqrt(jnp.mean(outputs * outputs, axis=-1, keepdims=True) + 1e-06)


def add_states(earlier, later):
    return earlier + later


def slot_numbers(route_flat):
    one_hot = (route_flat[:, None] == jnp.arange(EXPERTS, dtype=jnp.int32)[None, :]).astype(
        jnp.int32
    )
    earlier = jnp.cumsum(one_hot, axis=0) - one_hot
    return route_flat * CAP + jnp.sum(earlier * one_hot, axis=1)


def make_runner(expert_gate, expert_up, expert_down):

    def run_experts(received):
        gate_val = jnp.einsum(
            "necd,edf->necf", received, expert_gate, preferred_element_type=jnp.float32
        )
        up_val = jnp.einsum(
            "necd,edf->necf", received, expert_up, preferred_element_type=jnp.float32
        )
        hidden = (jax.nn.silu(gate_val) * up_val).astype(jnp.bfloat16)
        partial_value = jnp.einsum(
            "necf,efd->necd", hidden, expert_down, preferred_element_type=jnp.float32
        ).astype(jnp.bfloat16)
        groups = lax.axis_size("head")
        shape_now = partial_value.shape
        split = partial_value.reshape(
            shape_now[0], shape_now[1], shape_now[2], groups, shape_now[3] // groups
        )
        by_group = lax.all_to_all(split, "head", split_axis=3, concat_axis=3, tiled=True)
        summed = jnp.sum(by_group.astype(jnp.float32), axis=3)
        return lax.all_to_all(
            summed.astype(jnp.bfloat16), "seq", split_axis=0, concat_axis=0, tiled=True
        ).astype(summed.dtype)

    return run_experts


def body(
    tokens, attn_weight, attn_gain, moe_gain, routes, gates, expert_gate, expert_up, expert_down
):
    local_rows = tokens.shape[0]
    normed = rms_scale(tokens, attn_gain).astype(jnp.bfloat16)
    weights = lax.all_gather(attn_weight, "seq", axis=1, tiled=True)
    head_count = weights.shape[2] // HEAD_DIM
    projected = [
        jnp.dot(normed, weights[which], preferred_element_type=jnp.float32)
        .astype(jnp.bfloat16)
        .reshape(local_rows, head_count, HEAD_DIM)
        for which in range(3)
    ]
    query_rows, key_rows, value_rows = projected
    own_state = jnp.einsum("thd,the->hde", key_rows, value_rows, preferred_element_type=jnp.float32)
    prefix = prefix_2(own_state, "seq", add_states, jnp.zeros_like(own_state))
    inter_part = jnp.einsum(
        "thd,hde->the", query_rows.astype(jnp.float32), prefix, precision=PRECISE
    )
    scores = jnp.einsum("thd,shd->hts", query_rows, key_rows, preferred_element_type=jnp.float32)
    lower_mask = jnp.arange(local_rows)[:, None] >= jnp.arange(local_rows)[None, :]
    scores = jnp.where(lower_mask[None], scores, 0.0)
    intra_part = jnp.einsum(
        "hts,she->the", scores, value_rows.astype(jnp.float32), precision=PRECISE
    )
    attended = (
        head_norm(inter_part + intra_part)
        .reshape(local_rows, head_count * HEAD_DIM)
        .astype(jnp.bfloat16)
    )
    out_part = lax.dot_general(
        attended, weights[3], (((1,), (1,)), ((), ())), preferred_element_type=jnp.float32
    )
    residual = (
        tokens.astype(jnp.float32)
        + lax.psum(out_part.astype(jnp.bfloat16), "head").astype(jnp.float32)
    ).astype(jnp.bfloat16)
    moe_in = rms_scale(residual, moe_gain).astype(jnp.bfloat16)
    route_flat = routes.reshape(-1)
    slots = slot_numbers(route_flat)
    owners = lax.axis_size("seq")
    local_experts = expert_gate.shape[0]
    source_row = jnp.arange(route_flat.shape[0], dtype=jnp.int32) // TOPK
    run_experts = make_runner(expert_gate, expert_up, expert_down)
    outbound = (
        jnp.zeros((EXPERTS * CAP, moe_in.shape[1]), jnp.bfloat16).at[slots].set(moe_in[source_row])
    )
    outbound = outbound.reshape(owners, local_experts, CAP, moe_in.shape[1])
    returned = run_experts(lax.all_to_all(outbound, "seq", split_axis=0, concat_axis=0, tiled=True))
    arrived = returned.reshape(EXPERTS * CAP, -1)[slots].reshape(local_rows, TOPK, -1)
    moe_partial = jnp.einsum("tkd,tk->td", arrived, gates, precision=PRECISE)
    column_span = moe_partial.shape[1]
    residual_share = lax.dynamic_slice_in_dim(
        residual, lax.axis_index("head") * column_span, column_span, 1
    )
    mixed_share = (residual_share.astype(jnp.float32) + moe_partial).astype(jnp.bfloat16)
    return lax.all_gather(mixed_share, "head", axis=1, tiled=True)


def solution(mesh):
    return jax.shard_map(
        body,
        mesh=mesh,
        in_specs=(
            P(("grp", "seq"), None),
            P(None, "seq", "head"),
            P(),
            P(),
            P(("grp", "seq"), None),
            P(("grp", "seq"), None),
            P("seq", None, "head"),
            P("seq", None, "head"),
            P("seq", "head", None),
        ),
        out_specs=P(("grp", "seq"), None),
        check_vma=False,
    )
```

profile of v0, /device:TPU:0, one launch (start us, length us, event | category | flops | bytes accessed | tf_op | source)
XLA Modules:
  0.0 538.8 jit_solution(6225158763991145865)
XLA Ops:
  6.5 0.0 copy-start.1
  6.5 0.0 copy-start.4
  6.5 0.0 all-gather.3.cloned.1.call-start
  6.5 0.7 all-gather.3.cloned.1.call-update
  7.3 0.0 all-reduce.2.cloned.1.call-start
  7.3 0.8 copy.35
  8.1 0.1 eq.29
  8.2 0.1 eq.25
  8.3 18.0 %reduce-window.6 = s32[64,8,128]{2,1,0:T(8,128)S(1)} reduce-window(s32[64,8,128]{2,1,0:T(8,128)S(1)} %fusion.48, s32[]{:T(128)} %constant.64.clone.1), window={size=1x1x128 pad=0_0x0_0x127_0}, to_apply=%region_5.6 | reduce-window | flops 8323072 | bytes 524292 | tf_op jit(solution)/shard_map/reduce-window
  26.3 0.1 slice.32
  26.5 0.1 copy.37
  26.7 0.1 copy.38
  26.8 1.2 fusion.37
  28.0 0.7 broadcast_multiply_fusion
  28.7 0.1 broadcast_add_fusion
  28.9 132.4 %all-gather.3.cloned.1.call-done = bf16[4,2048,512]{2,1,0:T(8,128)(2,1)} async-done(((bf16[4,512,512]{2,1,0:T(8,128)(2,1)}), bf16[4,2048,512]{2,1,0:T(8,128)(2,1)}) %all-gather.3.cloned.1.call-update) | async-done | bytes 8388624 | tf_op jit(solution)/shard_map/all_gather | solution.py:82
  161.3 0.0 copy-done.1
  161.3 0.0 copy-done.4
  161.3 2.1 fusion.30
  163.4 0.1 copy.55
  163.5 2.1 fusion.33
  165.6 0.2 convolution_convert_fusion.1
  165.8 16.1 %all-gather = bf16[16,128,128]{2,1,0:T(8,128)(2,1)S(1)} all-gather(bf16[4,128,128]{2,1,0:T(8,128)(2,1)S(1)} %convolution_convert_fusion.1), channel_id=2, replica_groups=mesh['grp'=2,'seq'=4,'head'=4] {'seq'}, dimensions={0}, use_global_device_ids=true | all-gather | bytes 655360 | tf_op jit(solution)/shard_map/all_gather | solution.py:17
  182.0 0.5 while.14
  182.0 0.1 add_select_fusion.2
  182.1 0.1 add_select_fusion.2
  182.3 0.1 add_select_fusion.2
  182.4 0.1 add_select_fusion.2
  182.5 2.1 fusion.32
  184.6 0.0 copy-start.2
  184.6 0.4 fusion.50
  185.0 0.2 convolution_select_fusion
  185.2 0.4 multiply_reduce_fusion
  185.7 3.2 convolution_convert_fusion
  188.9 0.0 all-reduce.2.cloned.1.call-update
  188.9 0.1 fusion.46
  189.0 0.1 copy.34
  189.1 0.1 mul.89
  189.2 31.6 %all-reduce.2.cloned.1.call-done = bf16[128,2048]{1,0:T(8,128)(2,1)} async-done(((bf16[128,2048]{1,0:T(8,128)(2,1)}), bf16[128,2048]{1,0:T(8,128)(2,1)}) %all-reduce.2.cloned.1.call-update) | async-done | bytes 524304 | tf_op jit(solution)/shard_map/psum | solution.py:112
  220.8 1.3 fusion.34
  222.1 0.0 copy-done.2
  222.1 0.2 fusion.36
  222.3 23.3 %scatter_custom_fusion = bf16[1152,2048]{1,0:T(8,128)(2,1)} fusion(s32[1024]{0:T(1024)S(1)} %bitcast.134, bf16[128,2048]{1,0:T(8,128)(2,1)S(1)} %fusion.36, s32[1024]{0:T(1024)S(1)} %broadcast_clamp_fusion.1, bf16[]{:T(256)} %constant.73.clone.1), kind=kCustom, calls=%fused_computation.13 | custom fusion | bytes 4718594 | tf_op jit(solution)/shard_map/scatter | solution.py:122
  245.6 17.8 %reshape.156 = bf16[4,16,18,2048]{3,2,1,0:T(8,128)(2,1)} reshape(bf16[1152,2048]{1,0:T(8,128)(2,1)} %scatter_custom_fusion) | data formatting | bytes 9437184 | tf_op jit(solution)/shard_map/reshape | solution.py:124
  263.3 5.4 copy.39
  268.7 107.8 %all_to_all.15 = bf16[4,16,18,2048]{3,1,2,0:T(8,128)(2,1)S(1)} all-to-all(bf16[4,16,18,2048]{3,1,2,0:T(8,128)(2,1)S(1)} %copy.39), channel_id=1, replica_groups=mesh['grp'=2,'seq'=4,'head'=4] {'seq'}, dimensions={0} | all-to-all | bytes 9437184 | tf_op jit(solution)/shard_map/all_to_all | solution.py:125
  376.5 0.0 copy-start
  376.5 2.2 copy-done
  378.7 10.7 %fusion.4 = f32[16,4,18,256]{3,2,1,0:T(8,128)S(1)} fusion(bf16[16,2048,256]{2,1,0:T(8,128)(2,1)} %param.17, bf16[4,16,18,2048]{3,1,2,0:T(8,128)(2,1)S(1)} %all_to_all.15), kind=kOutput, calls=%fused_computation.8 | convolution fusion | flops 1207959552 | bytes 22675456 | tf_op jit(solution)/shard_map/necd,edf->necf/dot_general | solution.py:53
  389.5 18.6 %convert_bitcast_fusion = bf16[4,16,18,2048]{3,2,0,1:T(8,128)(2,1)} fusion(bf16[16,256,2048]{2,1,0:T(8,128)(2,1)} %param.19, f32[16,4,18,256]{3,2,1,0:T(8,128)S(1)} %fusion.4, bf16[16,2048,256]{2,1,0:T(8,128)(2,1)} %param.18, bf16[4,16,18,2048]{3,1,2,0:T(8,128)(2,1)} %copy-done), kind=kOutput, calls=%fused_computation.12 | convolution fusion | flops 2420047872 | bytes 44171264 | tf_op jit(solution)/shard_map/necf,efd->necd/dot_general | solution.py:60
  408.1 11.3 %reshape.192 = bf16[4,16,18,4,512]{4,3,2,0,1:T(4,128)(2,1)} reshape(bf16[4,16,18,2048]{3,2,0,1:T(8,128)(2,1)} %convert_bitcast_fusion) | data formatting | bytes 9437184 | tf_op jit(solution)/shard_map/reshape | solution.py:65
  419.4 5.0 copy.43
  424.3 57.2 %all_to_all.16 = bf16[4,16,18,4,512]{4,1,2,0,3:T(8,128)(2,1)} all-to-all(bf16[4,16,18,4,512]{4,1,2,0,3:T(8,128)(2,1)S(1)} %copy.43), channel_id=1, replica_groups=mesh['grp'=2,'seq'=4,'head'=4] {'head'}, dimensions={3} | all-to-all | bytes 9437184 | tf_op jit(solution)/shard_map/all_to_all | solution.py:68
  481.6 4.8 reduce_sum.55
  486.4 3.5 all-to-all-start.2
  489.9 0.0 copy-done.3
  489.9 0.1 copy.50
  490.0 28.3 %all-to-all-done.2 = bf16[4,16,18,512]{3,1,2,0:T(8,128)(2,1)S(1)} async-done(((bf16[4,16,18,512]{3,1,2,0:T(8,128)(2,1)}), bf16[4,16,18,512]{3,1,2,0:T(8,128)(2,1)S(1)}, u32[]{:S(2)}, u32[]{:S(2)}) %all-to-all-start.2) | async-done | bytes 1179680 | tf_op jit(solution)/shard_map/all_to_all | solution.py:70
  518.3 0.7 copy.45
  519.0 0.4 reshape.158
  519.4 4.0 gather_fusion
  523.4 1.0 fusion.41
  524.4 6.5 %all_gather.15 = bf16[128,2048]{1,0:T(8,128)(2,1)S(1)} all-gather(bf16[128,512]{1,0:T(8,128)(2,1)S(1)} %fusion.47), channel_id=1, replica_groups=mesh['grp'=2,'seq'=4,'head'=4] {'head'}, dimensions={1}, use_global_device_ids=true | all-gather | bytes 655360 | tf_op jit(solution)/shard_map/all_gather | solution.py:133
  530.9 0.8 copy.93
  (15 shorter events, 0.2 us)
Async XLA Ops:
  6.5 154.8 %copy-start.1 = (bf16[128,2048]{1,0:T(8,128)(2,1)S(1)}, bf16[128,2048]{1,0:T(8,128)(2,1)}, u32[]{:S(2)}) copy-start(bf16[128,2048]{1,0:T(8,128)(2,1)} %param.11) | copy-start | bytes 1572868
  6.5 154.8 %copy-start.4 = (f32[2048]{0:T(1024)S(1)}, f32[2048]{0:T(1024)}, u32[]{:S(2)}) copy-start(f32[2048]{0:T(1024)} %param.13) | copy-start | bytes 24580
  6.5 154.7 %all-gather.3.cloned.1.call-start = ((), (), s32[]{:S(2)}) async-start(), calls=%async_computation.3 | async-start | bytes 10485760 | tf_op jit(solution)/shard_map/all_gather | solution.py:82
  7.3 213.5 %all-reduce.2.cloned.1.call-start = ((), (), s32[]{:S(2)}) async-start(), calls=%async_computation.4 | async-start | bytes 1048576 | tf_op jit(solution)/shard_map/psum | solution.py:112
  184.6 37.5 %copy-start.2 = (f32[2048]{0:T(1024)S(1)}, f32[2048]{0:T(1024)}, u32[]{:S(2)}) copy-start(f32[2048]{0:T(1024)} %param.14) | copy-start | bytes 24580
  376.5 2.2 copy-start
  481.6 8.4 %copy-start.3 = (f32[128,8]{0,1:T(8,128)S(1)}, f32[128,8]{0,1:T(8,128)}, u32[]{:S(2)}) copy-start(f32[128,8]{0,1:T(8,128)} %param.16) | copy-start | bytes 12292
  486.4 31.9 %all-to-all-start.2 = ((bf16[4,16,18,512]{3,1,2,0:T(8,128)(2,1)}), bf16[4,16,18,512]{3,1,2,0:T(8,128)(2,1)S(1)}, u32[]{:S(2)}, u32[]{:S(2)}) async-start(bf16[4,16,18,512]{3,1,2,0:T(8,128)(2,1)} %reduce_sum.55), calls=%async_computation.2 | async-start | bytes 2359296 | tf_op jit(solution)/shard_map/all_to_all | solution.py:70
Sparse Core Ops, SparseCore 0:
  8.9 152.3 all-gather.2
  189.0 31.6 all-reduce.1
where the time goes:
time: 539 us
  waiting for transfers between devices  193 us (36%)
  blocking collectives  188 us (35%)
  local copies, waits for them, and re-layouts  72.5 us (13%)
  matrix products  41 us (8%)
  other arithmetic  27.1 us (5%)
  between operations  13.9 us (3%)
    all_gather x1, waiting for transfers between devices, body(): weights = lax.all_gather(attn_weight, 'seq', axis=1, tiled=True)  132 us
    all_to_all x1, blocking collectives, body(): lax.all_to_all(outbound, 'seq', split_axis=0, concat_axis=0, tiled=True)  108 us
    all_to_all x1, blocking collectives, run_experts(): lax.all_to_all(split, 'head', split_axis=3, concat_axis=3, tiled=True)  57.2 us
    psum x1, waiting for transfers between devices, body(): lax.psum(out_part.astype(jnp.bfloat16), 'head').astype(jnp.float32)  31.6 us
    all_to_all x1, waiting for transfers between devices, run_experts(): lax.all_to_all(summed.astype(jnp.bfloat16), 'seq', split_axis=0, concat_a...  28.3 us
    scatter x1, local copies, waits for them, and re-layouts, body(): jnp.zeros((EXPERTS * CAP, moe_in.shape[1]), jnp.bfloat16).at[slots]  23.3 us
    reshape x2, local copies, waits for them, and re-layouts, body(): outbound = outbound.reshape(owners, local_experts, CAP, moe_in.shape[1])  23.1 us
    dot_general x1, matrix products, run_experts(): jnp.einsum('necf,efd->necd', hidden, expert_down, preferred_element_type=...  18.6 us
  transfers between devices with their start and end apart: 3, of which 3 were waited for; matrix products, arithmetic and copies ran while one was open for 4% of the time, Pallas kernels for 0%

commit v1 on v0

--- a/solution.py
+++ b/solution.py
@@ -1,12 +1,17 @@
+import functools
+
 import jax
 import jax.numpy as jnp
 from jax import lax
+from jax.experimental import pallas as pl
+from jax.experimental.pallas import tpu as pltpu
 from jax.sharding import PartitionSpec as P
 
 HEAD_DIM = 128
 EXPERTS = 64
 TOPK = 8
 CAP = 18
+MESH = pl.DeviceIdType.MESH
 
 
 PRECISE = lax.Precision.HIGHEST
@@ -133,9 +138,321 @@
     return lax.all_gather(mixed_share, "head", axis=1, tiled=True)
 
 
+def swap_kernel(axis, modes, *refs):
+    count = len(modes)
+    ins, outs = refs[:count], refs[count : 2 * count]
+    send_sem, recv_sem, own_sem = refs[2 * count :]
+    peers, me = lax.axis_size(axis), lax.axis_index(axis)
+    barrier = pltpu.get_barrier_semaphore()
+    for step in range(1, peers):
+        pl.semaphore_signal(
+            barrier, inc=1, device_id={axis: lax.rem(me + step, peers)}, device_id_type=MESH
+        )
+    pl.semaphore_wait(barrier, peers - 1)
+    copies = []
+    for step in range(1, peers):
+        peer = lax.rem(me + step, peers)
+        for which in range(count):
+            source = ins[which].at[peer] if modes[which] else ins[which]
+            copy = pltpu.make_async_remote_copy(
+                src_ref=source,
+                dst_ref=outs[which].at[me],
+                send_sem=send_sem.at[which, step - 1],
+                recv_sem=recv_sem.at[which, step - 1],
+                device_id={axis: peer},
+                device_id_type=MESH,
+            )
+            copy.start()
+            copies.append(copy)
+    own = []
+    for which in range(count):
+        source = ins[which].at[me] if modes[which] else ins[which]
+        copy = pltpu.make_async_copy(source, outs[which].at[me], own_sem.at[which])
+        copy.start()
+        own.append(copy)
+    for copy in own:
+        copy.wait()
+    for copy in copies:
+        copy.wait()
+
+
+def swap(arrays, modes, axis, ident):
+    peers = lax.axis_size(axis)
+    shapes = [
+        jax.ShapeDtypeStruct(a.shape if mode else (peers,) + a.shape, a.dtype)
+        for a, mode in zip(arrays, modes)
+    ]
+    spec = pl.BlockSpec(memory_space=pltpu.VMEM)
+    return pl.pallas_call(
+        functools.partial(swap_kernel, axis, tuple(modes)),
+        out_shape=shapes,
+        in_specs=[spec] * len(arrays),
+        out_specs=[spec] * len(arrays),
+        scratch_shapes=[
+            pltpu.SemaphoreType.DMA((len(arrays), peers - 1)),
+            pltpu.SemaphoreType.DMA((len(arrays), peers - 1)),
+            pltpu.SemaphoreType.DMA((len(arrays),)),
+        ],
+        compiler_params=pltpu.CompilerParams(collective_id=ident, has_side_effects=True),
+    )(*arrays)
+
+
+def pair_of(me, bit):
+    side = lax.rem(me // bit, 2)
+    return side, me + bit * (1 - 2 * side)
+
+
+def pair_barrier(peer, axis):
+    barrier = pltpu.get_barrier_semaphore()
+    pl.semaphore_signal(barrier, inc=1, device_id={axis: peer}, device_id_type=MESH)
+    pl.semaphore_wait(barrier, 1)
+
+
+def pair_gather_kernel(axis, bit, x_ref, o_ref, send_sem, recv_sem, own_sem):
+    side, peer = pair_of(lax.axis_index(axis), bit)
+    pair_barrier(peer, axis)
+    copy = pltpu.make_async_remote_copy(
+        src_ref=x_ref,
+        dst_ref=o_ref.at[side],
+        send_sem=send_sem,
+        recv_sem=recv_sem,
+        device_id={axis: peer},
+        device_id_type=MESH,
+    )
+    copy.start()
+    own = pltpu.make_async_copy(x_ref, o_ref.at[side], own_sem)
+    own.start()
+    own.wait()
+    copy.wait()
+
+
+def pair_sum_kernel(axis, bit, x_ref, o_ref, held, send_sem, recv_sem):
+    side, peer = pair_of(lax.axis_index(axis), bit)
+    pair_barrier(peer, axis)
+    copy = pltpu.make_async_remote_copy(
+        src_ref=x_ref.at[1 - side],
+        dst_ref=held,
+        send_sem=send_sem,
+        recv_sem=recv_sem,
+        device_id={axis: peer},
+        device_id_type=MESH,
+    )
+    copy.start()
+    copy.wait()
+    for block in range(o_ref.shape[0]):
+        o_ref[block] = (
+            x_ref[side, block].astype(jnp.float32) + held[block].astype(jnp.float32)
+        ).astype(o_ref.dtype)
+
+
+def pair_call(kernel, x, axis, bit, shape, scratch, ident):
+    spec = pl.BlockSpec(memory_space=pltpu.VMEM)
+    return pl.pallas_call(
+        functools.partial(kernel, axis, bit),
+        out_shape=jax.ShapeDtypeStruct(shape, x.dtype),
+        in_specs=[spec],
+        out_specs=spec,
+        scratch_shapes=scratch,
+        compiler_params=pltpu.CompilerParams(collective_id=ident, has_side_effects=True),
+    )(x)
+
+
+def pair_gather(x, axis, bit, ident):
+    sem = pltpu.SemaphoreType.DMA
+    return pair_call(pair_gather_kernel, x, axis, bit, (2,) + x.shape, [sem, sem, sem], ident)
+
+
+def pair_sum(x, axis, bit, ident):
+    sem = pltpu.SemaphoreType.DMA
+    shape = x.shape[1:]
+    return pair_call(
+        pair_sum_kernel, x, axis, bit, shape, [pltpu.VMEM(shape, x.dtype), sem, sem], ident
+    )
+
+
+def gather_bits(x, axis, ident):
+    bits = lax.axis_size(axis).bit_length() - 1
+    own = x.shape
+    for k in reversed(range(bits)):
+        x = pair_gather(x, axis, 1 << k, ident + k)
+    x = x.transpose(tuple(reversed(range(bits))) + tuple(range(bits, x.ndim)))
+    return x.reshape((lax.axis_size(axis),) + own)
+
+
+def sum_bits(x, axis, ident):
+    bits = lax.axis_size(axis).bit_length() - 1
+    rest = x.shape[1:]
+    for k in range(bits):
+        left = x.shape[0] // 2
+        x = x.reshape((left, 2) + rest).transpose((1, 0) + tuple(range(2, 2 + len(rest))))
+        x = pair_sum(x, axis, 1 << k, ident + k)
+    return x[0]
+
+
+def moe_kernel(in_ref, pick_ref, mix_ref, gate_ref, up_ref, down_ref, o_ref, x_scr, y_scr):
+    expert = pl.program_id(0)
+    slots = x_scr.shape[0] // pl.num_programs(0)
+    span = o_ref.shape[2]
+
+    @pl.when(expert == 0)
+    def _():
+        for part in range(o_ref.shape[0]):
+            x_scr[:, part * span : (part + 1) * span] = jnp.dot(
+                pick_ref[...],
+                in_ref[:, part * span : (part + 1) * span],
+                preferred_element_type=jnp.float32,
+            ).astype(jnp.bfloat16)
+
+    rows = pl.ds(pl.multiple_of(expert * slots, slots), slots)
+    x = x_scr[rows, :]
+    gate_val = jnp.dot(x, gate_ref[0], preferred_element_type=jnp.float32)
+    up_val = jnp.dot(x, up_ref[0], preferred_element_type=jnp.float32)
+    hidden = (gate_val * jax.nn.sigmoid(gate_val) * up_val).astype(jnp.bfloat16)
+    y_scr[rows, :] = jnp.dot(hidden, down_ref[0], preferred_element_type=jnp.float32).astype(
+        jnp.bfloat16
+    )
+
+    @pl.when(expert == pl.num_programs(0) - 1)
+    def _():
+        for part in range(o_ref.shape[0]):
+            o_ref[part] = jnp.dot(
+                mix_ref[...],
+                y_scr[:, part * span : (part + 1) * span],
+                preferred_element_type=jnp.float32,
+            ).astype(jnp.bfloat16)
+
+
+def experts_here(moe_in, pick, mix, expert_gate, expert_up, expert_down, parts):
+    amount, wide, inner = expert_gate.shape
+    total = moe_in.shape[0]
+    fixed = lambda e: (0, 0)
+    one = lambda e: (e, 0, 0)
+    return pl.pallas_call(
+        moe_kernel,
+        out_shape=jax.ShapeDtypeStruct((parts, total, wide // parts), jnp.bfloat16),
+        grid=(amount,),
+        in_specs=[
+            pl.BlockSpec(moe_in.shape, fixed),
+            pl.BlockSpec(pick.shape, fixed),
+            pl.BlockSpec(mix.shape, fixed),
+            pl.BlockSpec((1, wide, inner), one),
+            pl.BlockSpec((1, wide, inner), one),
+            pl.BlockSpec((1, inner, wide), one),
+        ],
+        out_specs=pl.BlockSpec((parts, total, wide // parts), lambda e: (0, 0, 0)),
+        scratch_shapes=[
+            pltpu.VMEM((pick.shape[0], wide), jnp.bfloat16),
+            pltpu.VMEM((pick.shape[0], wide), jnp.bfloat16),
+        ],
+        compiler_params=pltpu.CompilerParams(dimension_semantics=("arbitrary",)),
+    )(moe_in, pick, mix, expert_gate, expert_up, expert_down)
+
+
+def slot_tables(route_rows, gate_rows, first, amount, slots):
+    total = route_rows.shape[1]
+    ids = (first + jnp.arange(amount)).astype(jnp.float32)
+    hit = route_rows[None] == ids[:, None, None]
+    named = jnp.any(hit, axis=1)
+    weight = jnp.sum(jnp.where(hit, gate_rows[None], 0.0), axis=1)
+    earlier = (jnp.arange(total)[:, None] < jnp.arange(total)[None, :]).astype(jnp.bfloat16)
+    rank = jnp.dot(named.astype(jnp.bfloat16), earlier, preferred_element_type=jnp.float32)
+    place = jnp.where(named, rank, -1.0)
+    spots = jnp.arange(slots, dtype=jnp.float32)
+    pick = (place[:, None, :] == spots[None, :, None]).astype(jnp.bfloat16)
+    pick = pick.reshape(amount * slots, total)
+    column = jnp.arange(amount * slots)
+    spread = (column[None, :] // slots == jnp.arange(amount)[:, None]).astype(jnp.bfloat16)
+    wide_place = lax.dot_general(
+        place.astype(jnp.bfloat16), spread, (((0,), (0,)), ((), ())),
+        preferred_element_type=jnp.float32,
+    )
+    wide_weight = lax.dot_general(
+        weight.astype(jnp.bfloat16), spread, (((0,), (0,)), ((), ())),
+        preferred_element_type=jnp.float32,
+    )
+    spot_of = (column % slots).astype(jnp.float32)
+    mix = jnp.where(wide_place == spot_of[None, :], wide_weight, 0.0).astype(jnp.bfloat16)
+    return pick, mix
+
+
+def token_body(
+    tokens, attn_weight, attn_gain, moe_gain, routes, gates, expert_gate, expert_up, expert_down
+):
+    local, width = tokens.shape
+    n_seq, n_head = lax.axis_size("seq"), lax.axis_size("head")
+    seq, head = lax.axis_index("seq"), lax.axis_index("head")
+    total = n_seq * local
+    depth, columns = attn_weight.shape[1:]
+    own_cols = columns // n_seq
+    wide_tokens = tokens.astype(jnp.float32)
+    factor = lax.rsqrt(jnp.mean(wide_tokens * wide_tokens, axis=-1) + 1e-06)
+    small = jnp.concatenate(
+        [routes.T.astype(jnp.float32), gates.T, jnp.broadcast_to(factor[None], (8, local))]
+    )
+    pieces = tokens.reshape(local, n_seq, depth).transpose(1, 0, 2)
+    piece_all, small_all = swap([pieces, small], [True, False], "seq", 1)
+    mine = piece_all.reshape(total, depth)
+    small_all = small_all.transpose(1, 0, 2).reshape(small.shape[0], total)
+    gain = lax.dynamic_slice_in_dim(attn_gain, seq * depth, depth)
+    normed = (
+        mine.astype(jnp.float32) * small_all[2 * TOPK][:, None] * gain[None]
+    ).astype(jnp.bfloat16)
+    part = [
+        jnp.dot(normed, attn_weight[which], preferred_element_type=jnp.float32)
+        .astype(jnp.bfloat16)
+        .reshape(total, n_seq, own_cols)
+        for which in range(3)
+    ]
+    part = jnp.stack(part).transpose(2, 0, 1, 3)
+    (part_all,) = swap([part], [True], "seq", 2)
+    joined = jnp.sum(part_all.astype(jnp.float32), axis=0).astype(jnp.bfloat16)
+    joined = joined.reshape(3, total, own_cols // HEAD_DIM, HEAD_DIM)
+    scores = jnp.einsum("thd,shd->hts", joined[0], joined[1], preferred_element_type=jnp.float32)
+    lower = jnp.arange(total)[:, None] >= jnp.arange(total)[None, :]
+    scores = jnp.where(lower[None], scores, 0.0).astype(jnp.bfloat16)
+    outputs = jnp.einsum("hts,she->the", scores, joined[2], preferred_element_type=jnp.float32)
+    attended = head_norm(outputs).astype(jnp.bfloat16).reshape(total, own_cols)
+    (attended_all,) = swap([attended], [False], "seq", 3)
+    attended_all = attended_all.transpose(1, 0, 2).reshape(total, columns)
+    out_part = lax.dot_general(
+        attended_all, attn_weight[3], (((1,), (1,)), ((), ())), preferred_element_type=jnp.float32
+    ).astype(jnp.bfloat16)
+    rows = total // n_head
+    out_sum = sum_bits(out_part.reshape(n_head, rows, depth), "head", 4)
+    kept = lax.dynamic_slice_in_dim(mine, head * rows, rows, 0)
+    residual_piece = (kept.astype(jnp.float32) + out_sum.astype(jnp.float32)).astype(jnp.bfloat16)
+    (residual_rows,) = swap([residual_piece], [False], "seq", 8)
+    residual = gather_bits(residual_rows, "head", 9)
+    residual = residual.transpose(0, 2, 1, 3).reshape(total, width)
+    moe_in = rms_scale(residual, moe_gain).astype(jnp.bfloat16)
+    amount = expert_gate.shape[0]
+    slots = -(-CAP * n_seq // 16) * 16
+    pick, mix = slot_tables(
+        small_all[:TOPK], small_all[TOPK : 2 * TOPK], seq * amount, amount, slots
+    )
+    sums = experts_here(moe_in, pick, mix, expert_gate, expert_up, expert_down, n_head)
+    share = sum_bits(sums, "head", 13)
+    (share_all,) = swap([share.reshape(n_seq, local, -1)], [True], "seq", 17)
+    moe_out = jnp.sum(share_all.astype(jnp.float32), axis=0)
+    span = moe_out.shape[1]
+    own_rows = lax.dynamic_slice(residual, (seq * local, head * span), (local, span))
+    mixed_share = (own_rows.astype(jnp.float32) + moe_out).astype(jnp.bfloat16)
+    mixed = gather_bits(mixed_share, "head", 18)
+    return mixed.transpose(1, 0, 2).reshape(local, width)
+
+
 def solution(mesh):
+    n_seq, n_head = mesh.shape["seq"], mesh.shape["head"]
+
+    def run(tokens, attn_weight, *rest):
+        heads_here = attn_weight.shape[2] // HEAD_DIM
+        power = n_head & (n_head - 1) == 0 and n_head > 1
+        if n_seq > 1 and power and heads_here % n_seq == 0:
+            return token_body(tokens, attn_weight, *rest)
+        return body(tokens, attn_weight, *rest)
+
     return jax.shard_map(
-        body,
+        run,
         mesh=mesh,
         in_specs=(
             P(("grp", "seq"), None),

time: 539 us -> 241 us (0.45)
  Pallas kernels: 0 us -> 198 us
  waiting for transfers between devices: 193 us -> 0 us
  blocking collectives: 188 us -> 0 us
  local copies, waits for them, and re-layouts: 72.5 us -> 17 us
  matrix products: 41 us -> 9.03 us
  between operations: 13.9 us -> 0.26 us
  other arithmetic: 27.1 us -> 15.9 us
    pallas_call x0 -> x14, Pallas kernels: none -> 198 us  [the longest x5 103 us: swap(): pl.pallas_call(functools.partial(swap_kernel, axis, tuple(modes)), out_sh...]
    all_to_all x2 -> x0, blocking collectives: 165 us -> none  [the longest x1 108 us: body(): lax.all_to_all(outbound, 'seq', split_axis=0, concat_axis=0, tiled=True)]
    all_gather x1 -> x0, waiting for transfers between devices: 132 us -> none  [body(): weights = lax.all_gather(attn_weight, 'seq', axis=1, tiled=True)]
    reshape x6 -> x3, local copies, waits for them, and re-layouts: 39.9 us -> 5.05 us  [the longest x1 3.02 us: sum_bits(): x.reshape((left, 2) + rest)]
    dot_general x11 -> x8, matrix products: 41 us -> 9.03 us  [the longest x3 4.58 us: token_body(): jnp.dot(normed, attn_weight[which], preferred_element_type=jnp.float32)]
    psum x1 -> x0, waiting for transfers between devices: 31.6 us -> none  [body(): lax.psum(out_part.astype(jnp.bfloat16), 'head').astype(jnp.float32)]
    all_to_all x1 -> x0, waiting for transfers between devices: 28.3 us -> none  [run_experts(): lax.all_to_all(summed.astype(jnp.bfloat16), 'seq', split_axis=0, concat_a...]
    scatter x1 -> x0, local copies, waits for them, and re-layouts: 23.3 us -> none  [body(): jnp.zeros((EXPERTS * CAP, moe_in.shape[1]), jnp.bfloat16).at[slots]]
  transfers between devices with their start and end apart: 3 -> 0, of which waited for: 3 -> 0; matrix products, arithmetic and copies ran while one was open for 4% -> 0% of each run, Pallas kernels for 0% -> 0%
where the time goes in v1:
time: 241 us; the launch traced here: 240 us
  Pallas kernels  198 us (82%)
  local copies, waits for them, and re-layouts  17 us (7%)
  other arithmetic  15.9 us (7%)
  matrix products  9.03 us (4%)
    pallas_call x5, Pallas kernels, swap(): pl.pallas_call(functools.partial(swap_kernel, axis, tuple(modes)), out_sh...  103 us
    pallas_call x8, Pallas kernels, pair_call(): pl.pallas_call(functools.partial(kernel, axis, bit), out_shape=jax.ShapeD...  62.7 us
    pallas_call x1, Pallas kernels, experts_here(): pl.pallas_call(moe_kernel, out_shape=jax.ShapeDtypeStruct((parts, total,...  31.9 us

profile of v1, /device:TPU:0, one launch (start us, length us, event | category | flops | bytes accessed | tf_op | source)
XLA Modules:
  0.0 239.9 jit_solution(6678369792358937833)
XLA Ops:
  0.0 1.2 multiply_reduce_fusion.1
  1.2 0.8 dynamic_slice.10
  2.0 0.7 convert_bitcast_fusion
  2.7 1.3 pad_maximum_fusion.refs_1_
  4.0 0.1 eq.71
  4.1 1.3 copy.37
  5.4 1.0 copy.38
  6.4 17.3 %shard_map.91 = (bf16[4,128,512]{2,1,0:T(8,128)(2,1)}, f32[4,24,128]{2,1,0:T(8,128)}) custom-call(bf16[4,128,512]{2,1,0:T(8,128)(2,1)} %bitcast.104, f32[24,128]{1,0:T(8,128)} %pad_maximum_fusion.refs_1_), custom_call_target="tpu_custom_call" | custom-call | tf_op jit(solution)/shard_map/pallas_call | solution.py:186
  23.7 0.7 slice.46
  24.4 0.7 slice_bitcast_fusion.8
  25.1 0.2 fusion.14
  25.3 0.2 compare_reduce_fusion
  25.5 0.2 convolution_select_fusion.2
  25.6 1.2 multiply_convert_fusion.1
  26.9 1.5 convolution_convert_fusion.1
  28.4 0.3 copy.41
  28.7 1.5 convolution_convert_fusion.2
  30.2 1.5 convolution_convert_fusion.3
  31.8 0.3 copy.39
  32.0 0.3 copy.40
  32.3 1.3 maximum_bitcast_fusion.refs_0_
  33.6 34.5 %shard_map.92 = bf16[4,3,512,128]{3,2,1,0:T(8,128)(2,1)} custom-call(bf16[4,3,512,128]{3,2,1,0:T(8,128)(2,1)} %maximum_bitcast_fusion.refs_0_), custom_call_target="tpu_custom_call" | custom-call | tf_op jit(solution)/shard_map/pallas_call | solution.py:186
  68.2 1.7 reduce_sum.58
  69.9 0.6 multiply_reduce_fusion.2
  70.5 0.8 fusion.16.refs_0_
  71.3 20.4 %shard_map.93 = bf16[4,512,128]{2,1,0:T(8,128)(2,1)} custom-call(bf16[512,128]{1,0:T(8,128)(2,1)} %fusion.16.refs_0_), custom_call_target="tpu_custom_call" | custom-call | tf_op jit(solution)/shard_map/pallas_call | solution.py:186
  91.7 1.2 copy.43
  93.0 1.5 convolution_convert_fusion
  94.5 0.8 copy.56
  95.3 3.3 %shard_map.94 = bf16[2,128,512]{2,1,0:T(8,128)(2,1)} custom-call(bf16[2,2,128,512]{3,2,1,0:T(8,128)(2,1)} %bitcast.105), custom_call_target="tpu_custom_call" | custom-call | tf_op jit(solution)/shard_map/pallas_call | solution.py:250
  98.7 7.2 %shard_map.95 = bf16[1,128,512]{2,1,0:T(8,128)(2,1)} custom-call(bf16[2,1,128,512]{3,2,1,0:T(8,128)(2,1)} %bitcast.110), custom_call_target="tpu_custom_call" | custom-call | tf_op jit(solution)/shard_map/pallas_call | solution.py:250
  105.9 1.7 fusion.15.refs_0_
  107.6 14.9 %shard_map.96.x_ref = bf16[4,128,512]{2,1,0:T(8,128)(2,1)} custom-call(bf16[128,512]{1,0:T(8,128)(2,1)} %fusion.15.refs_0_), custom_call_target="tpu_custom_call" | custom-call | tf_op jit(solution)/shard_map/pallas_call | solution.py:186
  122.5 15.3 %shard_map.97.x_ref = bf16[2,4,128,512]{3,2,1,0:T(8,128)(2,1)} custom-call(bf16[4,128,512]{2,1,0:T(8,128)(2,1)} %shard_map.96.x_ref), custom_call_target="tpu_custom_call" | custom-call | tf_op jit(solution)/shard_map/pallas_call | solution.py:250
  137.8 0.5 convolution_compare_fusion
  138.4 1.6 fusion.mix_ref
  139.9 5.3 %shard_map.98 = bf16[2,2,4,128,512]{4,3,2,1,0:T(8,128)(2,1)} custom-call(bf16[2,4,128,512]{3,2,1,0:T(8,128)(2,1)} %shard_map.97.x_ref), custom_call_target="tpu_custom_call" | custom-call | tf_op jit(solution)/shard_map/pallas_call | solution.py:250
  145.2 1.8 copy.45
  147.0 0.5 multiply_reduce_fusion
  147.5 1.4 fusion.1.pick_ref
  148.9 1.6 copy.46
  150.5 0.0 copy-start
  150.5 0.6 copy.52
  151.2 0.1 copy-done
  151.2 1.8 multiply_convert_fusion.in_ref
  153.1 31.9 %shard_map.99 = bf16[4,512,512]{2,1,0:T(8,128)(2,1)} custom-call(bf16[512,2048]{1,0:T(8,128)(2,1)} %multiply_convert_fusion.in_ref, bf16[1280,512]{1,0:T(8,128)(2,1)} %fusion.1.pick_ref, bf16[512,1280]{1,0:T(8,128)(2,1)} %fusion.mix_ref, bf16[16,2048,256]{2,1,0:T(8,128)(2,1)} %gate_ref.1, bf16[16,2048,256]{2,1,0:T(8,128)(2,1)} %up_ref.1, ...), custom_call_target="tpu_custom_call" | custom-call | tf_op jit(solution)/shard_map/pallas_call | solution.py:330
  185.0 3.0 %copy.55 = bf16[2,2,512,512]{3,2,0,1:T(8,128)(2,1)} copy(bf16[2,2,512,512]{3,2,1,0:T(8,128)(2,1)} %bitcast.97) | data formatting | bytes 4194304 | tf_op jit(solution)/shard_map/reshape | solution.py:287
  188.0 5.5 %shard_map.100 = bf16[2,512,512]{2,1,0:T(8,128)(2,1)} custom-call(bf16[2,2,512,512]{3,2,1,0:T(8,128)(2,1)} %bitcast.100), custom_call_target="tpu_custom_call" | custom-call | tf_op jit(solution)/shard_map/pallas_call | solution.py:250
  193.5 16.2 %shard_map.101 = bf16[1,512,512]{2,1,0:T(8,128)(2,1)} custom-call(bf16[2,1,512,512]{3,2,1,0:T(8,128)(2,1)} %bitcast.101), custom_call_target="tpu_custom_call" | custom-call | tf_op jit(solution)/shard_map/pallas_call | solution.py:250
  209.7 16.1 %shard_map.102 = bf16[4,128,512]{2,1,0:T(8,128)(2,1)} custom-call(bf16[4,128,512]{2,1,0:T(8,128)(2,1)} %bitcast.102), custom_call_target="tpu_custom_call" | custom-call | tf_op jit(solution)/shard_map/pallas_call | solution.py:186
  225.8 1.2 convert_reduce_fusion
  226.9 0.7 add_convert_fusion.x_ref
  227.6 6.6 %shard_map.103.x_ref = bf16[2,128,512]{2,1,0:T(8,128)(2,1)} custom-call(bf16[128,512]{1,0:T(8,128)(2,1)} %add_convert_fusion.x_ref), custom_call_target="tpu_custom_call" | custom-call | tf_op jit(solution)/shard_map/pallas_call | solution.py:250
  234.2 3.3 %shard_map.104 = bf16[2,2,128,512]{3,2,1,0:T(8,128)(2,1)} custom-call(bf16[2,128,512]{2,1,0:T(8,128)(2,1)} %shard_map.103.x_ref), custom_call_target="tpu_custom_call" | custom-call | tf_op jit(solution)/shard_map/pallas_call | solution.py:250
  237.6 1.1 copy.48
  238.6 0.3 copy.49
  238.9 1.0 copy.50
  (7 shorter events, 0.0 us)
Async XLA Ops:
  150.5 0.7 copy-start

commit v2 on v1

--- a/solution.py
+++ b/solution.py
@@ -208,24 +208,6 @@
     pl.semaphore_wait(barrier, 1)
 
 
-def pair_gather_kernel(axis, bit, x_ref, o_ref, send_sem, recv_sem, own_sem):
-    side, peer = pair_of(lax.axis_index(axis), bit)
-    pair_barrier(peer, axis)
-    copy = pltpu.make_async_remote_copy(
-        src_ref=x_ref,
-        dst_ref=o_ref.at[side],
-        send_sem=send_sem,
-        recv_sem=recv_sem,
-        device_id={axis: peer},
-        device_id_type=MESH,
-    )
-    copy.start()
-    own = pltpu.make_async_copy(x_ref, o_ref.at[side], own_sem)
-    own.start()
-    own.wait()
-    copy.wait()
-
-
 def pair_sum_kernel(axis, bit, x_ref, o_ref, held, send_sem, recv_sem):
     side, peer = pair_of(lax.axis_index(axis), bit)
     pair_barrier(peer, axis)
@@ -257,11 +239,6 @@
     )(x)
 
 
-def pair_gather(x, axis, bit, ident):
-    sem = pltpu.SemaphoreType.DMA
-    return pair_call(pair_gather_kernel, x, axis, bit, (2,) + x.shape, [sem, sem, sem], ident)
-
-
 def pair_sum(x, axis, bit, ident):
     sem = pltpu.SemaphoreType.DMA
     shape = x.shape[1:]
@@ -270,23 +247,212 @@
     )
 
 
-def gather_bits(x, axis, ident):
-    bits = lax.axis_size(axis).bit_length() - 1
-    own = x.shape
-    for k in reversed(range(bits)):
-        x = pair_gather(x, axis, 1 << k, ident + k)
-    x = x.transpose(tuple(reversed(range(bits))) + tuple(range(bits, x.ndim)))
-    return x.reshape((lax.axis_size(axis),) + own)
-
-
-def sum_bits(x, axis, ident):
-    bits = lax.axis_size(axis).bit_length() - 1
-    rest = x.shape[1:]
+def flip(index, bit):
+    return index + bit * (1 - 2 * lax.rem(index // bit, 2))
+
+
+def masked(index, mask):
+    bit = 1
+    while bit <= mask:
+        if mask & bit:
+            index = flip(index, bit)
+        bit *= 2
+    return index
+
+
+def below(mask, peers):
+    bits = [1 << k for k in reversed(range(peers.bit_length() - 1))]
+    return [bit for bit in bits if mask == 0 or bit < (mask & -mask)]
+
+
+def arrivals(peers):
+    order = [0]
+    for mask in order:
+        order.extend(mask + bit for bit in below(mask, peers))
+    return order
+
+
+def greet(axis_peers):
+    barrier = pltpu.get_barrier_semaphore()
+    for target in axis_peers:
+        pl.semaphore_signal(barrier, inc=1, device_id=target, device_id_type=MESH)
+    pl.semaphore_wait(barrier, len(axis_peers))
+
+
+def remote(source, dest, send_sem, recv_sem, target):
+    return pltpu.make_async_remote_copy(
+        src_ref=source,
+        dst_ref=dest,
+        send_sem=send_sem,
+        recv_sem=recv_sem,
+        device_id=target,
+        device_id_type=MESH,
+    )
+
+
+def spread_kernel(split, x_ref, o_ref, send_sem, recv_sem, own_sem):
+    n_seq, n_head = lax.axis_size("seq"), lax.axis_size("head")
+    seq, head = lax.axis_index("seq"), lax.axis_index("head")
+    rows, cols = x_ref.shape[-2:]
+    bits = [1 << k for k in range(n_head.bit_length() - 1)]
+
+    def place(head_at, seq_at):
+        if split:
+            return o_ref.at[seq_at, head_at]
+        return o_ref.at[
+            pl.ds(pl.multiple_of(head_at * rows, rows), rows),
+            pl.ds(pl.multiple_of(seq_at * cols, cols), cols),
+        ]
+
+    peers = [{"seq": lax.rem(seq + k, n_seq)} for k in range(1, n_seq)]
+    greet(peers + [{"head": flip(head, bit)} for bit in bits])
+    copies = {}
+    for k in range(1, n_seq):
+        to = lax.rem(seq + k, n_seq)
+        copies[0, k] = remote(
+            x_ref.at[to, head] if split else x_ref,
+            place(head, seq),
+            send_sem.at[0, k],
+            recv_sem.at[0, k],
+            {"seq": to},
+        )
+        copies[0, k].start()
+    if split:
+        own = pltpu.make_async_copy(x_ref.at[seq], o_ref.at[seq], own_sem)
+    else:
+        own = pltpu.make_async_copy(x_ref, place(head, seq), own_sem)
+    own.start()
+    for mask in arrivals(n_head):
+        for k in range(1 if split else 0, n_seq):
+            if (mask, k) in copies:
+                copies[mask, k].wait_recv()
+            block = place(masked(head, mask), lax.rem(seq + n_seq - k, n_seq))
+            source = x_ref if (mask, k) == (0, 0) else block
+            for bit in below(mask, n_head):
+                copy = remote(
+                    source,
+                    block,
+                    send_sem.at[mask + bit, k],
+                    recv_sem.at[mask + bit, k],
+                    {"head": flip(head, bit)},
+                )
+                copy.start()
+                copies[mask + bit, k] = copy
+    own.wait()
+    for copy in copies.values():
+        copy.wait_send()
+
+
+def spread(x, split, ident):
+    n_seq, n_head = lax.axis_size("seq"), lax.axis_size("head")
+    rows, cols = x.shape[-2:]
+    shape = x.shape if split else (n_head * rows, n_seq * cols)
+    sem = pltpu.SemaphoreType.DMA
+    spec = pl.BlockSpec(memory_space=pltpu.VMEM)
+    return pl.pallas_call(
+        functools.partial(spread_kernel, split),
+        out_shape=jax.ShapeDtypeStruct(shape, x.dtype),
+        in_specs=[spec],
+        out_specs=spec,
+        scratch_shapes=[sem((n_head, n_seq)), sem((n_head, n_seq)), sem],
+        compiler_params=pltpu.CompilerParams(collective_id=ident, has_side_effects=True),
+    )(x)
+
+
+def finish_kernel(
+    x_ref, keep_ref, o_ref, held, buf, got, share, pair_sems, seq_sems, head_sems, own_sem
+):
+    n_seq, n_head = lax.axis_size("seq"), lax.axis_size("head")
+    seq, head = lax.axis_index("seq"), lax.axis_index("head")
+    top = n_head // 2
+    side, peer = head // top, flip(head, top)
+    span = share.shape[1]
+    bits = [1 << k for k in range(n_head.bit_length() - 1)]
+    peers = [{"seq": lax.rem(seq + k, n_seq)} for k in range(1, n_seq)]
+    greet(peers + [{"head": flip(head, bit)} for bit in bits])
+    order = list(range(1, n_seq)) + [0]
+    firsts, swaps = {}, {}
+    for k in order:
+        to = lax.rem(seq + k, n_seq)
+        firsts[k] = remote(
+            x_ref.at[1 - side, to], held.at[k], pair_sems.at[0, k], pair_sems.at[1, k],
+            {"head": peer},
+        )
+        firsts[k].start()
+    for k in order:
+        to = lax.rem(seq + k, n_seq)
+        firsts[k].wait_recv()
+        value = x_ref[side, to].astype(jnp.float32) + held[k].astype(jnp.float32)
+        if k:
+            buf[k] = value.astype(buf.dtype)
+            swaps[k] = remote(
+                buf.at[k], got.at[k], seq_sems.at[0, k], seq_sems.at[1, k], {"seq": to}
+            )
+            swaps[k].start()
+        else:
+            total = value + keep_ref[...].astype(jnp.float32)
+    for k in range(1, n_seq):
+        swaps[k].wait_recv()
+        total = total + got[k].astype(jnp.float32)
+    share[...] = total.astype(share.dtype)
+
+    def place(head_at):
+        return o_ref.at[:, pl.ds(pl.multiple_of(head_at * span, span), span)]
+
+    copies = {}
+    for mask in arrivals(n_head):
+        if mask in copies:
+            copies[mask].wait_recv()
+        block = place(masked(head, mask))
+        for bit in below(mask, n_head):
+            copies[mask + bit] = remote(
+                block if mask else share,
+                block,
+                head_sems.at[0, mask + bit],
+                head_sems.at[1, mask + bit],
+                {"head": flip(head, bit)},
+            )
+            copies[mask + bit].start()
+    own = pltpu.make_async_copy(share, place(head), own_sem)
+    own.start()
+    own.wait()
+    for copy in (*firsts.values(), *swaps.values(), *copies.values()):
+        copy.wait_send()
+
+
+def finish(sums, keep, ident):
+    n_seq, n_head = lax.axis_size("seq"), lax.axis_size("head")
+    local, span = keep.shape
+    sem = pltpu.SemaphoreType.DMA
+    spec = pl.BlockSpec(memory_space=pltpu.VMEM)
+    blocks = pltpu.VMEM((n_seq, local, span), sums.dtype)
+    return pl.pallas_call(
+        finish_kernel,
+        out_shape=jax.ShapeDtypeStruct((local, n_head * span), keep.dtype),
+        in_specs=[spec] * 2,
+        out_specs=spec,
+        scratch_shapes=[
+            blocks,
+            blocks,
+            blocks,
+            pltpu.VMEM((local, span), keep.dtype),
+            sem((2, n_seq)),
+            sem((2, n_seq)),
+            sem((2, n_head)),
+            sem,
+        ],
+        compiler_params=pltpu.CompilerParams(collective_id=ident, has_side_effects=True),
+    )(sums, keep)
+
+
+def sum_bits(x, axis, bits, ident):
     for k in range(bits):
-        left = x.shape[0] // 2
-        x = x.reshape((left, 2) + rest).transpose((1, 0) + tuple(range(2, 2 + len(rest))))
-        x = pair_sum(x, axis, 1 << k, ident + k)
-    return x[0]
+        x = pair_sum(x.reshape((2, -1) + x.shape[-2:]), axis, 1 << k, ident + k)
+    return x
+
+
+def low_first(index, bits):
+    return sum(((index >> k) & 1) << (bits - 1 - k) for k in range(bits))
 
 
 def moe_kernel(in_ref, pick_ref, mix_ref, gate_ref, up_ref, down_ref, o_ref, x_scr, y_scr):
@@ -315,7 +481,8 @@
     @pl.when(expert == pl.num_programs(0) - 1)
     def _():
         for part in range(o_ref.shape[0]):
-            o_ref[part] = jnp.dot(
+            bits = o_ref.shape[0].bit_length() - 1
+            o_ref[low_first(part, bits)] = jnp.dot(
                 mix_ref[...],
                 y_scr[:, part * span : (part + 1) * span],
                 preferred_element_type=jnp.float32,
@@ -389,9 +556,9 @@
     small = jnp.concatenate(
         [routes.T.astype(jnp.float32), gates.T, jnp.broadcast_to(factor[None], (8, local))]
     )
-    pieces = tokens.reshape(local, n_seq, depth).transpose(1, 0, 2)
-    piece_all, small_all = swap([pieces, small], [True, False], "seq", 1)
-    mine = piece_all.reshape(total, depth)
+    pieces = tokens.reshape(n_head, local // n_head, n_seq, depth).transpose(2, 0, 1, 3)
+    (small_all,) = swap([small], [False], "seq", 1)
+    mine = spread(pieces, True, 2).reshape(total, depth)
     small_all = small_all.transpose(1, 0, 2).reshape(small.shape[0], total)
     gain = lax.dynamic_slice_in_dim(attn_gain, seq * depth, depth)
     normed = (
@@ -404,7 +571,7 @@
         for which in range(3)
     ]
     part = jnp.stack(part).transpose(2, 0, 1, 3)
-    (part_all,) = swap([part], [True], "seq", 2)
+    (part_all,) = swap([part], [True], "seq", 3)
     joined = jnp.sum(part_all.astype(jnp.float32), axis=0).astype(jnp.bfloat16)
     joined = joined.reshape(3, total, own_cols // HEAD_DIM, HEAD_DIM)
     scores = jnp.einsum("thd,shd->hts", joined[0], joined[1], preferred_element_type=jnp.float32)
@@ -412,18 +579,20 @@
     scores = jnp.where(lower[None], scores, 0.0).astype(jnp.bfloat16)
     outputs = jnp.einsum("hts,she->the", scores, joined[2], preferred_element_type=jnp.float32)
     attended = head_norm(outputs).astype(jnp.bfloat16).reshape(total, own_cols)
-    (attended_all,) = swap([attended], [False], "seq", 3)
+    (attended_all,) = swap([attended], [False], "seq", 4)
     attended_all = attended_all.transpose(1, 0, 2).reshape(total, columns)
     out_part = lax.dot_general(
         attended_all, attn_weight[3], (((1,), (1,)), ((), ())), preferred_element_type=jnp.float32
     ).astype(jnp.bfloat16)
     rows = total // n_head
-    out_sum = sum_bits(out_part.reshape(n_head, rows, depth), "head", 4)
+    bits = n_head.bit_length() - 1
+    out_part = jnp.stack(
+        [out_part[low_first(k, bits) * rows : (low_first(k, bits) + 1) * rows] for k in range(n_head)]
+    )
+    out_sum = sum_bits(out_part, "head", bits, 5).reshape(rows, depth)
     kept = lax.dynamic_slice_in_dim(mine, head * rows, rows, 0)
     residual_piece = (kept.astype(jnp.float32) + out_sum.astype(jnp.float32)).astype(jnp.bfloat16)
-    (residual_rows,) = swap([residual_piece], [False], "seq", 8)
-    residual = gather_bits(residual_rows, "head", 9)
-    residual = residual.transpose(0, 2, 1, 3).reshape(total, width)
+    residual = spread(residual_piece, False, 5 + bits)
     moe_in = rms_scale(residual, moe_gain).astype(jnp.bfloat16)
     amount = expert_gate.shape[0]
     slots = -(-CAP * n_seq // 16) * 16
@@ -431,14 +600,10 @@
         small_all[:TOPK], small_all[TOPK : 2 * TOPK], seq * amount, amount, slots
     )
     sums = experts_here(moe_in, pick, mix, expert_gate, expert_up, expert_down, n_head)
-    share = sum_bits(sums, "head", 13)
-    (share_all,) = swap([share.reshape(n_seq, local, -1)], [True], "seq", 17)
-    moe_out = jnp.sum(share_all.astype(jnp.float32), axis=0)
-    span = moe_out.shape[1]
+    span = width // n_head
+    pair = sum_bits(sums, "head", bits - 1, 6 + bits).reshape(2, n_seq, local, span)
     own_rows = lax.dynamic_slice(residual, (seq * local, head * span), (local, span))
-    mixed_share = (own_rows.astype(jnp.float32) + moe_out).astype(jnp.bfloat16)
-    mixed = gather_bits(mixed_share, "head", 18)
-    return mixed.transpose(1, 0, 2).reshape(local, width)
+    return finish(pair, own_rows, 6 + 2 * bits)
 
 
 def solution(mesh):

time: 241 us -> 213 us (0.88)
  Pallas kernels: 198 us -> 176 us
  local copies, waits for them, and re-layouts: 17 us -> 9.41 us
    pallas_call x0 -> x3, Pallas kernels: none -> 65 us  [the longest x2 36.7 us: spread(): pl.pallas_call(functools.partial(spread_kernel, split), out_shape=jax.Sha...]
    pallas_call x8 -> x3, Pallas kernels: 62.7 us -> 16.1 us  [pair_call(): pl.pallas_call(functools.partial(kernel, axis, bit), out_shape=jax.ShapeD...]
    pallas_call x5 -> x3, Pallas kernels: 103 us -> 63 us  [swap(): pl.pallas_call(functools.partial(swap_kernel, axis, tuple(modes)), out_sh...]
    transpose x4 -> x0, local copies, waits for them, and re-layouts: 4.76 us -> none  [the longest x2 2.87 us: gather_bits(): x = x.transpose(tuple(reversed(range(bits))) + tuple(range(bits, x.ndim)))]
    reshape x3 -> x2, local copies, waits for them, and re-layouts: 5.05 us -> 2.34 us  [token_body(): tokens.reshape(n_head, local // n_head, n_seq, depth).transpose(2, 0, 1, 3)]
where the time goes in v2:
time: 213 us; the launch traced here: 211 us
  Pallas kernels  176 us (83%)
  other arithmetic  16.6 us (8%)
  local copies, waits for them, and re-layouts  9.41 us (4%)
  matrix products  9.08 us (4%)
    pallas_call x3, Pallas kernels, swap(): pl.pallas_call(functools.partial(swap_kernel, axis, tuple(modes)), out_sh...  63 us
    pallas_call x2, Pallas kernels, spread(): pl.pallas_call(functools.partial(spread_kernel, split), out_shape=jax.Sha...  36.7 us
    pallas_call x1, Pallas kernels, experts_here(): pl.pallas_call(moe_kernel, out_shape=jax.ShapeDtypeStruct((parts, total,...  31.9 us
    pallas_call x1, Pallas kernels, finish(): pl.pallas_call(finish_kernel, out_shape=jax.ShapeDtypeStruct((local, n_he...  28.3 us
    pallas_call x3, Pallas kernels, pair_call(): pl.pallas_call(functools.partial(kernel, axis, bit), out_shape=jax.ShapeD...  16.1 us
    dot_general x3, matrix products, token_body(): jnp.dot(normed, attn_weight[which], preferred_element_type=jnp.float32)  4.58 us

profile of v2, /device:TPU:0, one launch (start us, length us, event | category | flops | bytes accessed | tf_op | source)
XLA Modules:
  0.0 211.3 jit_solution(14211461632888191222)
XLA Ops:
  0.0 1.2 multiply_reduce_fusion
  1.2 0.8 dynamic_slice.10
  2.0 0.7 convert_bitcast_fusion
  2.7 1.3 pad_maximum_fusion.1.refs_0_
  4.0 0.1 eq.71
  4.1 8.9 %shard_map.92 = f32[4,24,128]{2,1,0:T(8,128)} custom-call(f32[24,128]{1,0:T(8,128)} %pad_maximum_fusion.1.refs_0_), custom_call_target="tpu_custom_call" | custom-call | tf_op jit(solution)/shard_map/pallas_call | solution.py:186
  13.0 0.7 slice_reduce_fusion
  13.7 0.7 slice_bitcast_fusion.12
  14.4 0.2 fusion.17
  14.6 0.2 compare_reduce_fusion
  14.8 0.1 mul.76
  14.8 0.2 convolution_select_fusion.2
  15.0 1.4 reshape.160
  16.5 0.9 copy.25
  17.4 13.3 %shard_map.91 = bf16[4,4,32,512]{3,2,1,0:T(8,128)(2,1)} custom-call(bf16[4,4,32,512]{3,2,1,0:T(8,128)(2,1)} %bitcast.85), custom_call_target="tpu_custom_call" | custom-call | tf_op jit(solution)/shard_map/pallas_call | solution.py:352
  30.7 1.2 multiply_convert_fusion
  31.9 1.5 convolution_convert_fusion.1
  33.4 0.3 copy.20
  33.7 1.5 convolution_convert_fusion.2
  35.2 1.5 convolution_convert_fusion.3
  36.8 0.3 copy.18
  37.1 0.3 copy.19
  37.3 1.3 maximum_bitcast_fusion.refs_0_
  38.7 32.8 %shard_map.93 = bf16[4,3,512,128]{3,2,1,0:T(8,128)(2,1)} custom-call(bf16[4,3,512,128]{3,2,1,0:T(8,128)(2,1)} %maximum_bitcast_fusion.refs_0_), custom_call_target="tpu_custom_call" | custom-call | tf_op jit(solution)/shard_map/pallas_call | solution.py:186
  71.5 1.7 reduce_sum.49
  73.2 0.6 multiply_reduce_fusion.1
  73.8 0.8 fusion.19.refs_0_
  74.6 21.3 %shard_map.94 = bf16[4,512,128]{2,1,0:T(8,128)(2,1)} custom-call(bf16[512,128]{1,0:T(8,128)(2,1)} %fusion.19.refs_0_), custom_call_target="tpu_custom_call" | custom-call | tf_op jit(solution)/shard_map/pallas_call | solution.py:186
  96.0 1.2 copy.22
  97.2 1.5 convolution_convert_fusion
  98.8 0.9 pad_maximum_fusion
  99.7 3.3 %shard_map.95 = bf16[2,128,512]{2,1,0:T(8,128)(2,1)} custom-call(bf16[2,2,128,512]{3,2,1,0:T(8,128)(2,1)} %bitcast.84), custom_call_target="tpu_custom_call" | custom-call | tf_op jit(solution)/shard_map/pallas_call | solution.py:232
  103.0 7.2 %shard_map.96 = bf16[1,128,512]{2,1,0:T(8,128)(2,1)} custom-call(bf16[2,1,128,512]{3,2,1,0:T(8,128)(2,1)} %bitcast.86), custom_call_target="tpu_custom_call" | custom-call | tf_op jit(solution)/shard_map/pallas_call | solution.py:232
  110.2 1.7 fusion.18.x_ref
  111.9 0.5 convolution_compare_fusion
  112.4 1.6 fusion.3.mix_ref
  114.1 1.3 fusion.4.pick_ref
  115.4 0.0 copy-start.1
  115.4 23.4 %shard_map.97 = bf16[512,2048]{1,0:T(8,128)(2,1)} custom-call(bf16[128,512]{1,0:T(8,128)(2,1)} %fusion.18.x_ref), custom_call_target="tpu_custom_call" | custom-call | tf_op jit(solution)/shard_map/pallas_call | solution.py:352
  138.8 0.0 copy-start
  138.9 2.2 %fusion = f32[512]{0:T(512)S(1)} fusion(bf16[512,2048]{1,0:T(8,128)(2,1)} %shard_map.97), kind=kLoop, calls=%fused_computation.2 | loop fusion | flops 3145216 | bytes 2099200 | tf_op jit(solution)/shard_map/reduce_sum | solution.py:35
  141.1 0.0 copy-done
  141.1 0.7 dynamic_slice.11.keep_ref
  141.8 0.0 copy-done.1
  141.8 1.8 fusion.2.in_ref
  143.6 31.9 %shard_map.98 = bf16[4,512,512]{2,1,0:T(8,128)(2,1)} custom-call(bf16[512,2048]{1,0:T(8,128)(2,1)} %fusion.2.in_ref, bf16[1280,512]{1,0:T(8,128)(2,1)} %fusion.4.pick_ref, bf16[512,1280]{1,0:T(8,128)(2,1)} %fusion.3.mix_ref, bf16[16,2048,256]{2,1,0:T(8,128)(2,1)} %gate_ref.1, bf16[16,2048,256]{2,1,0:T(8,128)(2,1)} %up_ref.1, bf16[16,256,2048]{2,1,0:T(8,128)(2,1)} %down_ref.1), custom_call_target="tpu_custom_call" | custom-call | tf_op jit(solution)/shard_map/pallas_call | solution.py:497
  175.6 5.5 %shard_map.99 = bf16[2,512,512]{2,1,0:T(8,128)(2,1)} custom-call(bf16[2,2,512,512]{3,2,1,0:T(8,128)(2,1)} %bitcast.80), custom_call_target="tpu_custom_call" | custom-call | tf_op jit(solution)/shard_map/pallas_call | solution.py:232
  181.1 28.3 %shard_map.100 = bf16[128,2048]{1,0:T(8,128)(2,1)} custom-call(bf16[2,4,128,512]{3,2,1,0:T(8,128)(2,1)} %bitcast.81, bf16[128,512]{1,0:T(8,128)(2,1)} %dynamic_slice.11.keep_ref), custom_call_target="tpu_custom_call" | custom-call | tf_op jit(solution)/shard_map/pallas_call | solution.py:429
  209.4 1.9 copy.29
  (8 shorter events, 0.1 us)
Async XLA Ops:
  115.4 26.4 %copy-start.1 = (f32[2048]{0:T(1024)S(1)}, f32[2048]{0:T(1024)}, u32[]{:S(2)}) copy-start(f32[2048]{0:T(1024)} %param.12) | copy-start | bytes 24580
  138.8 2.2 %copy-start = (bf16[512,2048]{1,0:T(8,128)(2,1)S(1)}, bf16[512,2048]{1,0:T(8,128)(2,1)}, u32[]{:S(2)}) copy-start(bf16[512,2048]{1,0:T(8,128)(2,1)} %shard_map.97) | copy-start | bytes 6291460

commit v3 on v2

--- a/solution.py
+++ b/solution.py
@@ -290,7 +290,11 @@
     )
 
 
-def spread_kernel(split, x_ref, o_ref, send_sem, recv_sem, own_sem):
+def spread_kernel(split, *refs):
+    if split:
+        x_ref, t_ref, o_ref, to_ref, send_sem, recv_sem, own_sem, t_sems = refs
+    else:
+        x_ref, o_ref, send_sem, recv_sem, own_sem = refs
     n_seq, n_head = lax.axis_size("seq"), lax.axis_size("head")
     seq, head = lax.axis_index("seq"), lax.axis_index("head")
     rows, cols = x_ref.shape[-2:]
@@ -306,9 +310,14 @@
 
     peers = [{"seq": lax.rem(seq + k, n_seq)} for k in range(1, n_seq)]
     greet(peers + [{"head": flip(head, bit)} for bit in bits])
-    copies = {}
+    copies, tables = {}, []
     for k in range(1, n_seq):
         to = lax.rem(seq + k, n_seq)
+        if split:
+            tables.append(
+                remote(t_ref, to_ref.at[seq], t_sems.at[0, k], t_sems.at[1, k], {"seq": to})
+            )
+            tables[-1].start()
         copies[0, k] = remote(
             x_ref.at[to, head] if split else x_ref,
             place(head, seq),
@@ -339,22 +348,111 @@
                 copy.start()
                 copies[mask + bit, k] = copy
     own.wait()
+    if split:
+        own = pltpu.make_async_copy(t_ref, to_ref.at[seq], own_sem)
+        own.start()
+        own.wait()
+    for copy in tables:
+        copy.wait()
     for copy in copies.values():
         copy.wait_send()
 
 
-def spread(x, split, ident):
+def spread(x, split, ident, table=None):
     n_seq, n_head = lax.axis_size("seq"), lax.axis_size("head")
     rows, cols = x.shape[-2:]
     shape = x.shape if split else (n_head * rows, n_seq * cols)
+    shapes = [jax.ShapeDtypeStruct(shape, x.dtype)]
+    sem = pltpu.SemaphoreType.DMA
+    scratch = [sem((n_head, n_seq)), sem((n_head, n_seq)), sem]
+    args = [x]
+    if split:
+        args.append(table)
+        shapes.append(jax.ShapeDtypeStruct((n_seq,) + table.shape, table.dtype))
+        scratch.append(sem((2, n_seq)))
+    spec = pl.BlockSpec(memory_space=pltpu.VMEM)
+    return pl.pallas_call(
+        functools.partial(spread_kernel, split),
+        out_shape=shapes,
+        in_specs=[spec] * len(args),
+        out_specs=[spec] * len(args),
+        scratch_shapes=scratch,
+        compiler_params=pltpu.CompilerParams(collective_id=ident, has_side_effects=True),
+    )(*args)
+
+
+def swap_sum_kernel(x_ref, o_ref, got, total, hand, mixed, send_sem, recv_sem, extra_sems):
+    peers, me = lax.axis_size("seq"), lax.axis_index("seq")
+    last = peers - 1
+    greet([{"seq": lax.rem(me + k, peers)} for k in range(1, peers)])
+    relayed = peers >= 4
+    ends = (me == 0) | (me == last)
+    relay = (me == 1) | (me == last - 1)
+    near = jnp.where(me <= 1, 1 - me, 2 * last - 1 - me)
+    far = jnp.where(me <= 1, last, 0)
+    handed = remote(x_ref.at[far], hand, extra_sems.at[0], extra_sems.at[1], {"seq": near})
+    step_far = lax.rem(far - me + peers, peers)
+    passed = remote(mixed, got.at[step_far], extra_sems.at[2], recv_sem.at[step_far], {"seq": far})
+    if relayed:
+
+        @pl.when(ends)
+        def _():
+            handed.start()
+
+    copies, direct, coming = [], [], []
+    for k in range(1, peers):
+        to = lax.rem(me + k, peers)
+        copy = remote(x_ref.at[to], got.at[k], send_sem.at[k], recv_sem.at[k], {"seq": to})
+        plain = jnp.logical_not((ends | relay) & (to == far)) if relayed else me >= 0
+        copies.append(copy)
+        direct.append(plain)
+        source = lax.rem(me + peers - k, peers)
+        coming.append(jnp.logical_not(ends & (source + me == last)) if relayed else me >= 0)
+        pl.when(plain)(copy.start)
+    if relayed:
+
+        @pl.when(relay)
+        def _():
+            handed.wait_recv()
+            mixed[...] = (
+                hand[...].astype(jnp.float32) + x_ref[far].astype(jnp.float32)
+            ).astype(mixed.dtype)
+            passed.start()
+
+    total[...] = x_ref[me].astype(jnp.float32)
+    for k in range(1, peers):
+
+        @pl.when(coming[k - 1])
+        def _():
+            copies[k - 1].wait_recv()
+            total[...] += got[k].astype(jnp.float32)
+
+    o_ref[...] = total[...].astype(o_ref.dtype)
+    for copy, plain in zip(copies, direct):
+        pl.when(plain)(copy.wait_send)
+    if relayed:
+        pl.when(ends)(handed.wait_send)
+        pl.when(relay)(passed.wait_send)
+
+
+def swap_sum(x, ident):
+    peers, block = x.shape[0], x.shape[1:]
     sem = pltpu.SemaphoreType.DMA
     spec = pl.BlockSpec(memory_space=pltpu.VMEM)
     return pl.pallas_call(
-        functools.partial(spread_kernel, split),
-        out_shape=jax.ShapeDtypeStruct(shape, x.dtype),
+        swap_sum_kernel,
+        out_shape=jax.ShapeDtypeStruct(block, x.dtype),
         in_specs=[spec],
         out_specs=spec,
-        scratch_shapes=[sem((n_head, n_seq)), sem((n_head, n_seq)), sem],
+        scratch_shapes=[
+            pltpu.VMEM(x.shape, x.dtype),
+            pltpu.VMEM(block, jnp.float32),
+            pltpu.VMEM(block, x.dtype),
+            pltpu.VMEM(block, x.dtype),
+            sem((peers,)),
+            sem((peers,)),
+            sem((3,)),
+        ],
         compiler_params=pltpu.CompilerParams(collective_id=ident, has_side_effects=True),
     )(x)
 
@@ -557,8 +655,8 @@
         [routes.T.astype(jnp.float32), gates.T, jnp.broadcast_to(factor[None], (8, local))]
     )
     pieces = tokens.reshape(n_head, local // n_head, n_seq, depth).transpose(2, 0, 1, 3)
-    (small_all,) = swap([small], [False], "seq", 1)
-    mine = spread(pieces, True, 2).reshape(total, depth)
+    mine, small_all = spread(pieces, True, 2, small)
+    mine = mine.reshape(total, depth)
     small_all = small_all.transpose(1, 0, 2).reshape(small.shape[0], total)
     gain = lax.dynamic_slice_in_dim(attn_gain, seq * depth, depth)
     normed = (
@@ -571,8 +669,7 @@
         for which in range(3)
     ]
     part = jnp.stack(part).transpose(2, 0, 1, 3)
-    (part_all,) = swap([part], [True], "seq", 3)
-    joined = jnp.sum(part_all.astype(jnp.float32), axis=0).astype(jnp.bfloat16)
+    joined = swap_sum(part.reshape(n_seq, 3 * total, own_cols), 3)
     joined = joined.reshape(3, total, own_cols // HEAD_DIM, HEAD_DIM)
     scores = jnp.einsum("thd,shd->hts", joined[0], joined[1], preferred_element_type=jnp.float32)
     lower = jnp.arange(total)[:, None] >= jnp.arange(total)[None, :]
@@ -592,7 +689,7 @@
     out_sum = sum_bits(out_part, "head", bits, 5).reshape(rows, depth)
     kept = lax.dynamic_slice_in_dim(mine, head * rows, rows, 0)
     residual_piece = (kept.astype(jnp.float32) + out_sum.astype(jnp.float32)).astype(jnp.bfloat16)
-    residual = spread(residual_piece, False, 5 + bits)
+    (residual,) = spread(residual_piece, False, 5 + bits)
     moe_in = rms_scale(residual, moe_gain).astype(jnp.bfloat16)
     amount = expert_gate.shape[0]
     slots = -(-CAP * n_seq // 16) * 16

time: 213 us -> 198 us (0.930)
  Pallas kernels: 176 us -> 162 us
    pallas_call x3 -> x1, Pallas kernels: 63 us -> 14.7 us  [swap(): pl.pallas_call(functools.partial(swap_kernel, axis, tuple(modes)), out_sh...]
    pallas_call x2 -> x3, Pallas kernels: 36.7 us -> 70.9 us  [the longest x2 38.2 us: spread(): pl.pallas_call(functools.partial(spread_kernel, split), out_shape=shapes,...]
where the time goes in v3:
time: 198 us; the launch traced here: 197 us
  Pallas kernels  162 us (82%)
  other arithmetic  14.8 us (7%)
  matrix products  10.1 us (5%)
  local copies, waits for them, and re-layouts  9.4 us (5%)
    pallas_call x2, Pallas kernels, spread(): pl.pallas_call(functools.partial(spread_kernel, split), out_shape=shapes,...  38.2 us
    pallas_call x1, Pallas kernels, swap_sum(): pl.pallas_call(swap_sum_kernel, out_shape=jax.ShapeDtypeStruct(block, x.d...  32.7 us
    pallas_call x1, Pallas kernels, experts_here(): pl.pallas_call(moe_kernel, out_shape=jax.ShapeDtypeStruct((parts, total,...  31.9 us
    pallas_call x1, Pallas kernels, finish(): pl.pallas_call(finish_kernel, out_shape=jax.ShapeDtypeStruct((local, n_he...  28.3 us
    pallas_call x3, Pallas kernels, pair_call(): pl.pallas_call(functools.partial(kernel, axis, bit), out_shape=jax.ShapeD...  16.1 us
    pallas_call x1, Pallas kernels, swap(): pl.pallas_call(functools.partial(swap_kernel, axis, tuple(modes)), out_sh...  14.7 us
    dot_general x3, matrix products, token_body(): jnp.dot(normed, attn_weight[which], preferred_element_type=jnp.float32)  4.58 us

profile of v3, /device:TPU:0, one launch (start us, length us, event | category | flops | bytes accessed | tf_op | source)
XLA Modules:
  0.0 196.5 jit_solution(13283314444940058332)
XLA Ops:
  0.0 1.2 multiply_reduce_fusion
  1.2 0.8 dynamic_slice.10
  2.0 0.7 convert_bitcast_fusion
  2.7 1.3 pad_maximum_fusion.2.refs_1_
  4.0 0.1 eq.71
  4.1 1.4 reshape.157
  5.5 0.9 copy.28
  6.4 16.3 %shard_map.91 = (bf16[4,4,32,512]{3,2,1,0:T(8,128)(2,1)}, f32[4,24,128]{2,1,0:T(8,128)}) custom-call(bf16[4,4,32,512]{3,2,1,0:T(8,128)(2,1)} %bitcast.68, f32[24,128]{1,0:T(8,128)} %pad_maximum_fusion.2.refs_1_), custom_call_target="tpu_custom_call" | custom-call | tf_op jit(solution)/shard_map/pallas_call | solution.py:374
  22.7 0.7 slice_reduce_fusion
  23.4 0.7 slice_bitcast_fusion.4
  24.2 0.2 fusion.17
  24.3 0.2 compare_reduce_fusion
  24.5 0.1 mul.76
  24.6 0.2 convolution_select_fusion.2
  24.8 1.2 multiply_convert_fusion
  26.0 1.5 convolution_convert_fusion.1
  27.5 0.3 copy.23
  27.8 1.5 convolution_convert_fusion.2
  29.3 1.5 convolution_convert_fusion.3
  30.9 0.3 copy.21
  31.1 0.3 copy.22
  31.4 1.3 pad_maximum_fusion
  32.8 32.7 %shard_map.92 = bf16[1536,128]{1,0:T(8,128)(2,1)} custom-call(bf16[4,1536,128]{2,1,0:T(8,128)(2,1)} %bitcast.65), custom_call_target="tpu_custom_call" | custom-call | tf_op jit(solution)/shard_map/pallas_call | solution.py:442
  65.4 1.6 multiply_reduce_fusion.1
  67.1 0.8 fusion.19.refs_0_
  67.9 14.7 %shard_map.93 = bf16[4,512,128]{2,1,0:T(8,128)(2,1)} custom-call(bf16[512,128]{1,0:T(8,128)(2,1)} %fusion.19.refs_0_), custom_call_target="tpu_custom_call" | custom-call | tf_op jit(solution)/shard_map/pallas_call | solution.py:186
  82.6 1.2 copy.25
  83.9 1.5 convolution_convert_fusion
  85.5 0.9 pad_maximum_fusion.1
  86.3 3.3 %shard_map.94 = bf16[2,128,512]{2,1,0:T(8,128)(2,1)} custom-call(bf16[2,2,128,512]{3,2,1,0:T(8,128)(2,1)} %bitcast.69), custom_call_target="tpu_custom_call" | custom-call | tf_op jit(solution)/shard_map/pallas_call | solution.py:232
  89.7 7.2 %shard_map.95 = bf16[1,128,512]{2,1,0:T(8,128)(2,1)} custom-call(bf16[2,1,128,512]{3,2,1,0:T(8,128)(2,1)} %bitcast.70), custom_call_target="tpu_custom_call" | custom-call | tf_op jit(solution)/shard_map/pallas_call | solution.py:232
  96.9 1.7 fusion.18.refs_0_
  98.6 0.5 convolution_compare_fusion
  99.1 1.6 fusion.3.mix_ref
  100.8 1.3 fusion.4.pick_ref
  102.1 0.0 copy-start.1
  102.1 21.9 %shard_map.96 = bf16[512,2048]{1,0:T(8,128)(2,1)} custom-call(bf16[128,512]{1,0:T(8,128)(2,1)} %fusion.18.refs_0_), custom_call_target="tpu_custom_call" | custom-call | tf_op jit(solution)/shard_map/pallas_call | solution.py:374
  124.1 0.0 copy-start
  124.1 2.2 %fusion = f32[512]{0:T(512)S(1)} fusion(bf16[512,2048]{1,0:T(8,128)(2,1)} %shard_map.96), kind=kLoop, calls=%fused_computation.2 | loop fusion | flops 3145216 | bytes 2099200 | tf_op jit(solution)/shard_map/reduce_sum | solution.py:35
  126.3 0.0 copy-done
  126.3 0.7 dynamic_slice.11.keep_ref
  127.0 0.0 copy-done.1
  127.0 1.8 fusion.2.in_ref
  128.8 31.9 %shard_map.97 = bf16[4,512,512]{2,1,0:T(8,128)(2,1)} custom-call(bf16[512,2048]{1,0:T(8,128)(2,1)} %fusion.2.in_ref, bf16[1280,512]{1,0:T(8,128)(2,1)} %fusion.4.pick_ref, bf16[512,1280]{1,0:T(8,128)(2,1)} %fusion.3.mix_ref, bf16[16,2048,256]{2,1,0:T(8,128)(2,1)} %gate_ref.1, bf16[16,2048,256]{2,1,0:T(8,128)(2,1)} %up_ref.1, bf16[16,256,2048]{2,1,0:T(8,128)(2,1)} %down_ref.1), custom_call_target="tpu_custom_call" | custom-call | tf_op jit(solution)/shard_map/pallas_call | solution.py:595
  160.8 5.5 %shard_map.98 = bf16[2,512,512]{2,1,0:T(8,128)(2,1)} custom-call(bf16[2,2,512,512]{3,2,1,0:T(8,128)(2,1)} %bitcast.64), custom_call_target="tpu_custom_call" | custom-call | tf_op jit(solution)/shard_map/pallas_call | solution.py:232
  166.3 28.3 %shard_map.99 = bf16[128,2048]{1,0:T(8,128)(2,1)} custom-call(bf16[2,4,128,512]{3,2,1,0:T(8,128)(2,1)} %bitcast.66, bf16[128,512]{1,0:T(8,128)(2,1)} %dynamic_slice.11.keep_ref), custom_call_target="tpu_custom_call" | custom-call | tf_op jit(solution)/shard_map/pallas_call | solution.py:527
  194.6 1.9 copy.32
  (8 shorter events, 0.1 us)
Async XLA Ops:
  102.1 24.9 %copy-start.1 = (f32[2048]{0:T(1024)S(1)}, f32[2048]{0:T(1024)}, u32[]{:S(2)}) copy-start(f32[2048]{0:T(1024)} %param.12) | copy-start | bytes 24580
  124.1 2.2 %copy-start = (bf16[512,2048]{1,0:T(8,128)(2,1)S(1)}, bf16[512,2048]{1,0:T(8,128)(2,1)}, u32[]{:S(2)}) copy-start(bf16[512,2048]{1,0:T(8,128)(2,1)} %shard_map.96) | copy-start | bytes 6291460
